TPU v7x, 128 devices: a whole 4x4x4 slice. The times are simulated.
128 devices in a mesh: expert: 8 (over z, core), fsdp: 16 (over y, x).
Axes of the slice: x: 4, y: 4, z: 4, core: 2. Of those that a mesh axis runs over, the one named last changes fastest.
Arguments:
- tokens: bfloat16 [32768, 2048], P(('expert', 'fsdp')), may hold values from -6 to 6
- expert_ids: int32 [32768, 6], P(('expert', 'fsdp')), may hold values from 0 to 63, as said below
- gate_vals: bfloat16 [32768, 6], P(('expert', 'fsdp')), may hold values from 0.099609375 to 1
- w_gate: bfloat16 [8, 2048, 1408], P('expert', 'fsdp'), may hold values from -0.125 to 0.125
- w_up: bfloat16 [8, 2048, 1408], P('expert', 'fsdp'), may hold values from -0.125 to 0.125
- w_down: bfloat16 [8, 2048, 1408], P('expert', 'fsdp'), may hold values from -0.15625 to 0.15625
- cotangent: bfloat16 [32768, 2048], P(('expert', 'fsdp')), may hold values from -6 to 6
Outputs:
- output: bfloat16 [32768, 2048], P(('expert', 'fsdp'))
- grad_tokens: bfloat16 [32768, 2048], P(('expert', 'fsdp'))
- grad_gates: float32 [32768, 6], P(('expert', 'fsdp'))
- grad_w_gate: float32 [8, 2048, 1408], P('expert', 'fsdp')
- grad_w_up: float32 [8, 2048, 1408], P('expert', 'fsdp')
- grad_w_down: float32 [8, 2048, 1408], P('expert', 'fsdp')
Inputs may be any that keep to these rules, and one draw needn't show every extreme that they name: `expert_ids`: each row names 6 different experts. Among the tokens of one device at most 48 name any one expert whose number modulo 8 is below 1. On every device some such expert is named by exactly 48 of its tokens, and for every column one such expert is named by exactly 48 tokens of every device of that column.
All inputs are finite; a program needn't handle non-finite values.
Results may differ from a plain program's by a relative error of at most 0.013.
Values may be sent and summed in bfloat16 or wider, within the bound.
No kernel may reach another device: no remote copies, remote signals or barrier semaphores. Data moves between devices by JAX's collectives and lax.ppermute only.
A program may use at most 128 MiB of HBM per device.

v0:
```python
import jax
import jax.numpy as jnp
from jax import lax
from jax.sharding import PartitionSpec as P

EXPERTS = 64
TOP = 6
WAVE = 1
MOST = 48


def slot_tables(expert_ids, groups):
    per_index = EXPERTS // groups
    window = WAVE * groups
    tok_count = expert_ids.shape[0]
    flat_ids = expert_ids.reshape(-1)
    local_index = flat_ids % per_index
    is_live = local_index < WAVE
    window_slot = jnp.where(is_live, flat_ids // per_index * WAVE + local_index, window)
    onehot = (window_slot[:, None] == jnp.arange(window, dtype=jnp.int32)[None, :]).astype(
        jnp.int32
    )
    rank_in = jnp.sum((jnp.cumsum(onehot, axis=0) - 1) * onehot, axis=1)
    target = jnp.where(is_live, window_slot * MOST + rank_in, window * MOST)
    slot_ids = jnp.arange(tok_count * TOP, dtype=jnp.int32)
    source = (
        jnp.full((window * MOST,), tok_count * TOP, jnp.int32).at[target].set(slot_ids, mode="drop")
    )
    return (target, source)


def on_device(tokens, expert_ids, gate_vals, w_gate, w_up, w_down, cotangent):
    groups = lax.axis_size("expert")
    tok_count, model_width = tokens.shape
    target, source = slot_tables(expert_ids, groups)
    token_of = source // TOP
    zero_row = jnp.zeros((1, model_width), jnp.bfloat16)
    tokens_pad = jnp.concatenate([tokens, zero_row], axis=0)
    cot_pad = jnp.concatenate([cotangent, zero_row], axis=0)
    gate_pad = jnp.concatenate([gate_vals.reshape(-1), jnp.zeros((1,), jnp.bfloat16)], axis=0)
    send_rows = tokens_pad[token_of].reshape(groups, WAVE * MOST, model_width)
    arrived = lax.all_to_all(send_rows, "expert", split_axis=0, concat_axis=0, tiled=True)
    rows_in = arrived.reshape(groups, WAVE, MOST, model_width)
    full_gate, full_up, full_down = (
        lax.all_gather(w_gate, "fsdp", axis=1, tiled=True),
        lax.all_gather(w_up, "fsdp", axis=1, tiled=True),
        lax.all_gather(w_down, "fsdp", axis=1, tiled=True),
    )
    gate_pre = jnp.einsum("skmd,kdf->skmf", rows_in, full_gate, preferred_element_type=jnp.float32)
    up_pre = jnp.einsum("skmd,kdf->skmf", rows_in, full_up, preferred_element_type=jnp.float32)
    sigmoid_g = jax.nn.sigmoid(gate_pre)
    hidden = (gate_pre * sigmoid_g * up_pre).astype(jnp.bfloat16)
    expert_out = jnp.einsum(
        "skmf,kdf->skmd", hidden, full_down, preferred_element_type=jnp.float32
    ).astype(jnp.bfloat16)
    returned = lax.all_to_all(
        expert_out.reshape(groups, WAVE * MOST, model_width),
        "expert",
        split_axis=0,
        concat_axis=0,
        tiled=True,
    )
    back_pad = jnp.concatenate([returned.reshape(-1, model_width), zero_row], axis=0)
    slot_out = back_pad[target].reshape(tok_count, TOP, model_width).astype(jnp.float32)
    output = jnp.sum(gate_vals.astype(jnp.float32)[:, :, None] * slot_out, axis=1).astype(
        jnp.bfloat16
    )
    grad_gates = jnp.sum(cotangent.astype(jnp.float32)[:, None, :] * slot_out, axis=2)
    gate_rows = gate_pad[source].astype(jnp.float32)
    send_grad = (gate_rows[:, None] * cot_pad[token_of].astype(jnp.float32)).astype(jnp.bfloat16)
    grad_in = lax.all_to_all(
        send_grad.reshape(groups, WAVE * MOST, model_width),
        "expert",
        split_axis=0,
        concat_axis=0,
        tiled=True,
    )
    out_grad = grad_in.reshape(groups, WAVE, MOST, model_width)
    hidden_grad = jnp.einsum(
        "skmd,kdf->skmf", out_grad, full_down, preferred_element_type=jnp.float32
    )
    gate_grad = (hidden_grad * up_pre * sigmoid_g * (1.0 + gate_pre * (1.0 - sigmoid_g))).astype(
        jnp.bfloat16
    )
    up_grad = (hidden_grad * gate_pre * sigmoid_g).astype(jnp.bfloat16)
    row_grad = (
        jnp.einsum("skmf,kdf->skmd", gate_grad, full_gate, preferred_element_type=jnp.float32)
        + jnp.einsum("skmf,kdf->skmd", up_grad, full_up, preferred_element_type=jnp.float32)
    ).astype(jnp.bfloat16)
    grads_home = lax.all_to_all(
        row_grad.reshape(groups, WAVE * MOST, model_width),
        "expert",
        split_axis=0,
        concat_axis=0,
        tiled=True,
    )
    grads_pad = jnp.concatenate([grads_home.reshape(-1, model_width), zero_row], axis=0)
    grad_tokens = jnp.sum(
        grads_pad[target].reshape(tok_count, TOP, model_width).astype(jnp.float32), axis=1
    ).astype(jnp.bfloat16)
    term_gate = jnp.einsum("skmd,skmf->kdf", rows_in, gate_grad, preferred_element_type=jnp.float32)
    term_up = jnp.einsum("skmd,skmf->kdf", rows_in, up_grad, preferred_element_type=jnp.float32)
    term_down = jnp.einsum("skmd,skmf->kdf", out_grad, hidden, preferred_element_type=jnp.float32)
    grad_w_gate, grad_w_up, grad_w_down = (
        lax.psum_scatter(
            term_gate.astype(jnp.bfloat16), "fsdp", scatter_dimension=1, tiled=True
        ).astype(jnp.float32),
        lax.psum_scatter(
            term_up.astype(jnp.bfloat16), "fsdp", scatter_dimension=1, tiled=True
        ).astype(jnp.float32),
        lax.psum_scatter(
            term_down.astype(jnp.bfloat16), "fsdp", scatter_dimension=1, tiled=True
        ).astype(jnp.float32),
    )
    return (output, grad_tokens, grad_gates, grad_w_gate, grad_w_up, grad_w_down)


def solution(mesh):
    placed = (
        P(("expert", "fsdp"), None),
        P(("expert", "fsdp"), None),
        P(("expert", "fsdp"), None),
        P("expert", "fsdp", None),
        P("expert", "fsdp", None),
        P("expert", "fsdp", None),
        P(("expert", "fsdp"), None),
    )
    return jax.shard_map(
        on_device,
        mesh=mesh,
        in_specs=placed,
        out_specs=(
            P(("expert", "fsdp"), None),
            P(("expert", "fsdp"), None),
            P(("expert", "fsdp"), None),
            P("expert", "fsdp", None),
            P("expert", "fsdp", None),
            P("expert", "fsdp", None),
        ),
        check_vma=False,
    )
```

profile of v0, /device:TPU:0, one launch (start us, length us, event | category | flops | bytes accessed | tf_op | source)
XLA Modules:
  0.0 461.0 jit_solution(18036882781366785138)
XLA Ops:
  14.7 6.2 %scatter_custom_fusion = s32[384]{0:T(512)S(1)} fusion(s32[1536]{0:T(1024)S(1)} %get-tuple-element.15, s32[1536]{0:T(1024)S(1)} %iota.11, s32[]{:T(128)} %constant.52.clone.1), kind=kCustom, calls=%fused_computation.94 | custom fusion | bytes 1540 | tf_op jit(solution)/shard_map/scatter | solution.py:27
  27.9 5.4 %all-to-all-start.2 = ((bf16[8,48,2048]{2,1,0:T(8,128)(2,1)}), bf16[8,48,2048]{2,1,0:T(8,128)(2,1)S(1)}, u32[]{:S(2)}, u32[]{:S(2)}) async-start(bf16[8,48,2048]{2,1,0:T(8,128)(2,1)} %fusion.15), calls=%async_computation.2 | async-start | bytes 3145728 | tf_op jit(solution)/shard_map/all_to_all | solution.py:71
  37.7 17.1 %all-to-all-done.2 = bf16[8,48,2048]{2,1,0:T(8,128)(2,1)S(1)} async-done(((bf16[8,48,2048]{2,1,0:T(8,128)(2,1)}), bf16[8,48,2048]{2,1,0:T(8,128)(2,1)S(1)}, u32[]{:S(2)}, u32[]{:S(2)}) %all-to-all-start.2) | async-done | bytes 1572896 | tf_op jit(solution)/shard_map/all_to_all | solution.py:71
  58.5 12.8 %all-gather.8.cloned.1.call-done = bf16[1,2048,1408]{2,1,0:T(8,128)(2,1)} async-done(((bf16[1,128,1408]{2,1,0:T(8,128)(2,1)}), bf16[1,2048,1408]{2,1,0:T(8,128)(2,1)}) %all-gather.8.cloned.1.call-update) | async-done | bytes 5767184 | tf_op jit(solution)/shard_map/all_gather | solution.py:47
  71.4 6.6 %fusion.22 = f32[8,1,48,1408]{3,2,0,1:T(8,128)} fusion(bf16[8,48,2048]{2,1,0:T(8,128)(2,1)S(1)} %all-to-all-done.2, bf16[1,2048,1408]{2,1,0:T(8,128)(2,1)} %all-gather.8.cloned.1.call-done), kind=kOutput, calls=%fused_computation.31 | convolution fusion | flops 2214592512 | bytes 9502720 | tf_op jit(solution)/shard_map/skmd,kdf->skmf/dot_general | solution.py:79
  80.0 52.0 %all-gather.6.cloned.1.call-done = bf16[1,2048,1408]{2,1,0:T(8,128)(2,1)} async-done(((bf16[1,128,1408]{2,1,0:T(8,128)(2,1)}), bf16[1,2048,1408]{2,1,0:T(8,128)(2,1)}) %all-gather.6.cloned.1.call-update) | async-done | bytes 5767184 | tf_op jit(solution)/shard_map/all_gather | solution.py:46
  132.0 6.6 %fusion.19 = f32[8,1,48,1408]{3,2,0,1:T(8,128)} fusion(bf16[8,48,2048]{2,1,0:T(8,128)(2,1)S(1)} %all-to-all-done, bf16[1,2048,1408]{2,1,0:T(8,128)(2,1)} %all-gather.6.cloned.1.call-done), kind=kOutput, calls=%fused_computation.30 | convolution fusion | flops 2214592512 | bytes 9502720 | tf_op jit(solution)/shard_map/skmd,kdf->skmf/dot_general | solution.py:50
  138.6 54.0 %all-gather.4.cloned.1.call-done = bf16[1,2048,1408]{2,1,0:T(8,128)(2,1)} async-done(((bf16[1,128,1408]{2,1,0:T(8,128)(2,1)}), bf16[1,2048,1408]{2,1,0:T(8,128)(2,1)}) %all-gather.4.cloned.1.call-update) | async-done | bytes 5767184 | tf_op jit(solution)/shard_map/all_gather | solution.py:45
  192.6 7.9 %multiply_convert_fusion.1 = (bf16[8,1,48,1408]{3,2,0,1:T(8,128)(2,1)}, bf16[8,1,48,1408]{3,2,0,1:T(8,128)(2,1)S(1)}, bf16[8,1,48,1408]{3,2,0,1:T(8,128)(2,1)}) fusion(f32[8,1,48,1408]{3,2,0,1:T(8,128)} %fusion.22, f32[8,1,48,1408]{3,2,0,1:T(8,128)} %fusion.19, bf16[8,48,2048]{2,1,0:T(8,128)(2,1)S(1)} %all-to-all-done, ...), kind=kOutput, calls=%fused_computation.34 | convolution fusion | flops 2223243264 | bytes 14909440 | tf_op jit(solution)/shard_map/skmd,kdf->skmf/dot_general | solution.py:49
  201.5 5.2 %fusion.2 = bf16[1,2048,1408]{2,1,0:T(8,128)(2,1)} fusion(bf16[8,48,2048]{2,1,0:T(8,128)(2,1)S(1)} %all-to-all-done.2, bf16[8,1,48,1408]{3,2,0,1:T(8,128)(2,1)S(1)} %get-tuple-element.17), kind=kOutput, calls=%fused_computation.13 | convolution fusion | flops 2217476096 | bytes 8421376 | tf_op jit(solution)/shard_map/skmd,skmf->kdf/dot_general | solution.py:103
  207.9 5.1 %fusion = bf16[1,2048,1408]{2,1,0:T(8,128)(2,1)} fusion(bf16[8,48,2048]{2,1,0:T(8,128)(2,1)S(1)} %all-to-all-done, bf16[8,1,48,1408]{3,2,0,1:T(8,128)(2,1)S(1)} %copy-done.7), kind=kOutput, calls=%fused_computation.11 | convolution fusion | flops 2217476096 | bytes 8421376 | tf_op jit(solution)/shard_map/skmd,skmf->kdf/dot_general | solution.py:101
  214.3 5.1 %fusion.1 = bf16[1,2048,1408]{2,1,0:T(8,128)(2,1)} fusion(bf16[8,48,2048]{2,1,0:T(8,128)(2,1)S(1)} %all-to-all-done, bf16[8,1,48,1408]{3,2,0,1:T(8,128)(2,1)S(1)} %copy-done.4), kind=kOutput, calls=%fused_computation.12 | convolution fusion | flops 2217476096 | bytes 8421376 | tf_op jit(solution)/shard_map/skmd,skmf->kdf/dot_general | solution.py:102
  220.6 7.8 %fusion.27 = bf16[8,48,2048]{2,1,0:T(8,128)(2,1)} fusion(bf16[1,2048,1408]{2,1,0:T(8,128)(2,1)} %all-gather.8.cloned.1.call-done, bf16[8,1,48,1408]{3,2,0,1:T(8,128)(2,1)S(1)} %copy-done.6), kind=kOutput, calls=%fused_computation.32 | convolution fusion | flops 2215378944 | bytes 8421376 | tf_op jit(solution)/shard_map/skmf,kdf->skmd/dot_general | solution.py:53
  232.9 5.2 %fusion.7 = f32[8,48,2048]{2,1,0:T(8,128)S(1)} fusion(bf16[1,2048,1408]{2,1,0:T(8,128)(2,1)} %all-gather.6.cloned.1.call-done, bf16[8,1,48,1408]{3,2,0,1:T(8,128)(2,1)} %get-tuple-element.18), kind=kOutput, calls=%fused_computation.18 | convolution fusion | flops 2214592512 | bytes 9994240 | tf_op jit(solution)/shard_map/skmf,kdf->skmd/dot_general | solution.py:88
  242.0 12.5 %all-to-all-done.1 = bf16[8,48,2048]{2,1,0:T(8,128)(2,1)S(1)} async-done(((bf16[8,48,2048]{2,1,0:T(8,128)(2,1)}), bf16[8,48,2048]{2,1,0:T(8,128)(2,1)S(1)}, u32[]{:S(2)}, u32[]{:S(2)}) %all-to-all-start.1) | async-done | bytes 1572896 | tf_op jit(solution)/shard_map/all_to_all | solution.py:56
  260.8 19.6 %all-to-all-done.3 = bf16[8,48,2048]{2,1,0:T(8,128)(2,1)} async-done(((bf16[8,48,2048]{2,1,0:T(8,128)(2,1)}), bf16[8,48,2048]{2,1,0:T(8,128)(2,1)}, u32[]{:S(2)}, u32[]{:S(2)}) %all-to-all-start.3) | async-done | bytes 1572896 | tf_op jit(solution)/shard_map/all_to_all | solution.py:90
  281.9 7.1 %gather_fusion.4 = bf16[1536,2048]{1,0:T(8,128)(2,1)} fusion(bf16[385,2048]{1,0:T(8,128)(2,1)S(1)} %concatenate.19, s32[2048]{0:T(1024)S(1)} %pad_clamp_fusion), kind=kCustom, calls=%fused_computation.4 | custom fusion | bytes 12589056 | tf_op jit(solution)/shard_map/gather | solution.py:99
  289.0 11.0 %reshape.325 = bf16[256,6,2048]{2,1,0:T(8,128)(2,1)} reshape(bf16[1536,2048]{1,0:T(8,128)(2,1)} %gather_fusion.4) | data formatting | bytes 12582912 | tf_op jit(solution)/shard_map/reshape | solution.py:99
  300.0 9.7 %reduce_sum.44 = bf16[256,2048]{1,0:T(8,128)(2,1)} reduce(bf16[256,6,2048]{2,1,0:T(8,128)(2,1)} %reshape.325, bf16[]{:T(256)} %constant.31.clone.1), dimensions={1}, to_apply=%region_5.6 | reduce | flops 2621440 | bytes 7340034 | tf_op jit(solution)/shard_map/reduce_sum | solution.py:98
  309.8 7.1 %gather_fusion.1 = bf16[1536,2048]{1,0:T(8,128)(2,1)} fusion(bf16[385,2048]{1,0:T(8,128)(2,1)S(1)} %concatenate.16, s32[2048]{0:T(1024)S(1)} %pad_clamp_fusion), kind=kCustom, calls=%fused_computation.1 | custom fusion | bytes 12589056 | tf_op jit(solution)/shard_map/gather | solution.py:64
  316.9 12.0 %reshape.326 = f32[256,6,2048]{2,1,0:T(8,128)} reshape(bf16[1536,2048]{1,0:T(8,128)(2,1)} %gather_fusion.1) | data formatting | bytes 18874368 | tf_op jit(solution)/shard_map/convert_element_type | solution.py:64
  328.9 11.9 %multiply_reduce_fusion = (f32[256,6]{1,0:T(8,128)S(1)}, bf16[256,2048]{1,0:T(8,128)(2,1)}) fusion(f32[256,6,2048]{2,1,0:T(8,128)} %reshape.326, f32[256,2048]{1,0:T(8,128)S(1)} %copy-done, f32[256,6]{1,0:T(8,128)S(1)} %copy.19), kind=kLoop, calls=%fused_computation.6 | loop fusion | flops 12057088 | bytes 15740928 | tf_op jit(solution)/shard_map/reduce_sum | solution.py:68
  343.4 26.1 %reduce-scatter.4.cloned.1.call-done = bf16[1,128,1408]{2,1,0:T(8,128)(2,1)} async-done(((bf16[1,2048,1408]{2,1,0:T(8,128)(2,1)}), bf16[1,128,1408]{2,1,0:T(8,128)(2,1)}) %reduce-scatter.4.cloned.1.call-update) | async-done | bytes 360464 | tf_op jit(solution)/shard_map/reduce_scatter | solution.py:105
  371.4 80.9 %reduce-scatter.6.cloned.1.call-done = bf16[1,128,1408]{2,1,0:T(8,128)(2,1)} async-done(((bf16[1,2048,1408]{2,1,0:T(8,128)(2,1)}), bf16[1,128,1408]{2,1,0:T(8,128)(2,1)}) %reduce-scatter.6.cloned.1.call-update) | async-done | bytes 360464 | tf_op jit(solution)/shard_map/reduce_scatter | solution.py:108
  (76 shorter events, 51.6 us)
Async XLA Ops:
  7.2 16.6 %copy-start.1 = (bf16[256,2048]{1,0:T(8,128)(2,1)S(1)}, bf16[256,2048]{1,0:T(8,128)(2,1)}, u32[]{:S(2)}) copy-start(bf16[256,2048]{1,0:T(8,128)(2,1)} %param.13) | copy-start | bytes 3145732
  7.2 64.2 %all-gather.8.cloned.1.call-start = ((), (), s32[]{:S(2)}) async-start(), calls=%async_computation.9 | async-start | bytes 6127616 | tf_op jit(solution)/shard_map/all_gather | solution.py:47
  7.9 124.1 %all-gather.6.cloned.1.call-start = ((), (), s32[]{:S(2)}) async-start(), calls=%async_computation.8 | async-start | bytes 6127616 | tf_op jit(solution)/shard_map/all_gather | solution.py:46
  8.7 184.0 %all-gather.4.cloned.1.call-start = ((), (), s32[]{:S(2)}) async-start(), calls=%async_computation.7 | async-start | bytes 6127616 | tf_op jit(solution)/shard_map/all_gather | solution.py:45
  27.9 27.0 %all-to-all-start.2 = ((bf16[8,48,2048]{2,1,0:T(8,128)(2,1)}), bf16[8,48,2048]{2,1,0:T(8,128)(2,1)S(1)}, u32[]{:S(2)}, u32[]{:S(2)}) async-start(bf16[8,48,2048]{2,1,0:T(8,128)(2,1)} %fusion.15), calls=%async_computation.2 | async-start | bytes 3145728 | tf_op jit(solution)/shard_map/all_to_all | solution.py:71
  54.9 25.1 %all-to-all-start = ((bf16[8,48,2048]{2,1,0:T(8,128)(2,1)}), bf16[8,48,2048]{2,1,0:T(8,128)(2,1)S(1)}, u32[]{:S(2)}, u32[]{:S(2)}) async-start(bf16[8,48,2048]{2,1,0:T(8,128)(2,1)} %bitcast.1), calls=%async_computation | async-start | bytes 3145728 | tf_op jit(solution)/shard_map/all_to_all | solution.py:42
  58.5 283.0 %reduce-scatter.8.cloned.1.call-start = ((), (), s32[]{:S(2)}) async-start(), calls=%async_computation.12 | async-start | bytes 6127616 | tf_op jit(solution)/shard_map/reduce_scatter | solution.py:111
  200.5 1.0 copy-start.5
  206.7 1.2 copy-start.7
  206.7 162.8 %reduce-scatter.4.cloned.1.call-start = ((), (), s32[]{:S(2)}) async-start(), calls=%async_computation.10 | async-start | bytes 6127616 | tf_op jit(solution)/shard_map/reduce_scatter | solution.py:105
  213.0 1.2 copy-start.4
  213.1 239.2 %reduce-scatter.6.cloned.1.call-start = ((), (), s32[]{:S(2)}) async-start(), calls=%async_computation.11 | async-start | bytes 6127616 | tf_op jit(solution)/shard_map/reduce_scatter | solution.py:108
  219.4 1.2 copy-start.6
  228.4 9.8 %slice-start = ((s8[5767168]{0:T(1024)(128)(4,1)}), s8[1572864]{0:T(1024)(128)(4,1)S(1)}, s32[]{:S(2)}) async-start(s8[5767168]{0:T(1024)(128)(4,1)} %bitcast.111), calls=%async_computation.13 | async-start | bytes 3145728
  228.4 26.1 %all-to-all-start.1 = ((bf16[8,48,2048]{2,1,0:T(8,128)(2,1)}), bf16[8,48,2048]{2,1,0:T(8,128)(2,1)S(1)}, u32[]{:S(2)}, u32[]{:S(2)}) async-start(bf16[8,48,2048]{2,1,0:T(8,128)(2,1)} %fusion.27), calls=%async_computation.1 | async-start | bytes 3145728 | tf_op jit(solution)/shard_map/all_to_all | solution.py:56
  232.9 5.2 %slice-start.1 = ((s8[5767168]{0:T(1024)(128)(4,1)}), s8[4194304]{0:T(1024)(128)(4,1)S(1)}, s32[]{:S(2)}) async-start(s8[5767168]{0:T(1024)(128)(4,1)} %bitcast.111), calls=%async_computation.14 | async-start | bytes 8388608
  232.9 5.2 %copy-start.8 = (bf16[8,1,48,1408]{3,2,0,1:T(8,128)(2,1)S(1)}, bf16[8,1,48,1408]{3,2,0,1:T(8,128)(2,1)}, u32[]{:S(2)}) copy-start(bf16[8,1,48,1408]{3,2,0,1:T(8,128)(2,1)} %get-tuple-element.16) | copy-start | bytes 3244036
  242.0 16.8 %copy-start.3 = (bf16[256,6]{0,1:T(8,128)(2,1)S(1)}, bf16[256,6]{0,1:T(8,128)(2,1)}, u32[]{:S(2)}) copy-start(bf16[256,6]{0,1:T(8,128)(2,1)} %param.9) | copy-start | bytes 9220
  242.0 16.9 %copy-start.2 = (bf16[256,2048]{1,0:T(8,128)(2,1)S(1)}, bf16[256,2048]{1,0:T(8,128)(2,1)}, u32[]{:S(2)}) copy-start(bf16[256,2048]{1,0:T(8,128)(2,1)} %param.13) | copy-start | bytes 3145732
  254.5 25.9 %all-to-all-start.3 = ((bf16[8,48,2048]{2,1,0:T(8,128)(2,1)}), bf16[8,48,2048]{2,1,0:T(8,128)(2,1)}, u32[]{:S(2)}, u32[]{:S(2)}) async-start(bf16[8,48,2048]{2,1,0:T(8,128)(2,1)} %add_convert_fusion), calls=%async_computation.3 | async-start | bytes 3145728 | tf_op jit(solution)/shard_map/all_to_all | solution.py:90
  316.9 12.0 %copy-start = (f32[256,2048]{1,0:T(8,128)S(1)}, f32[256,2048]{1,0:T(8,128)}, u32[]{:S(2)}) copy-start(f32[256,2048]{1,0:T(8,128)} %convert_element_type.110) | copy-start | bytes 6291460
Sparse Core Ops, SparseCore 0:
  10.1 61.1 all-gather.7
  73.5 58.4 all-gather.5
  134.1 58.4 all-gather.3
  206.8 79.7 reduce-scatter.7
  289.8 79.5 reduce-scatter.3
  372.7 79.5 reduce-scatter.5
where the time goes:
time: 463 us; the launch traced here: 461 us
  waiting for transfers between devices  279 us (60%)
  local copies, waits for them, and re-layouts  62.6 us (14%)
  matrix products  53.3 us (12%)
  other arithmetic  33.2 us (7%)
  starting transfers between devices  18.3 us (4%)
  between operations  14.4 us (3%)
    reduce_scatter x1, waiting for transfers between devices, on_device(): lax.psum_scatter(term_up.astype(jnp.bfloat16), 'fsdp', scatter_dimension=...  80.9 us
    all_gather x1, waiting for transfers between devices, on_device(): lax.all_gather(w_gate, 'fsdp', axis=1, tiled=True)  54 us
    all_gather x1, waiting for transfers between devices, on_device(): lax.all_gather(w_up, 'fsdp', axis=1, tiled=True)  52 us
    reduce_scatter x1, waiting for transfers between devices, on_device(): lax.psum_scatter(term_gate.astype(jnp.bfloat16), 'fsdp', scatter_dimensio...  26.1 us
    all_to_all x1, waiting for transfers between devices, on_device(): lax.all_to_all(row_grad.reshape(groups, WAVE * MOST, model_width), 'exper...  19.6 us
    all_to_all x1, waiting for transfers between devices, on_device(): lax.all_to_all(send_grad.reshape(groups, WAVE * MOST, model_width), 'expe...  17.1 us
    all_gather x1, waiting for transfers between devices, on_device(): lax.all_gather(w_down, 'fsdp', axis=1, tiled=True)  12.8 us
    all_to_all x1, waiting for transfers between devices, on_device(): lax.all_to_all(expert_out.reshape(groups, WAVE * MOST, model_width), 'exp...  12.5 us
  transfers between devices with their start and end apart: 10, of which 9 were waited for; matrix products, arithmetic and copies ran while one was open for 28% of the time, Pallas kernels for 0%

commit v1 on v0

--- a/solution.py
+++ b/solution.py
@@ -7,6 +7,11 @@
 TOP = 6
 WAVE = 1
 MOST = 48
+
+
+def _number_series_all(array_in, mesh_dim):
+    kept_arr = jnp.concatenate([array_in] * lax.axis_size(mesh_dim), axis=1)
+    return lax.all_to_all(kept_arr, axis_name=mesh_dim, split_axis=1, concat_axis=1, tiled=True)
 
 
 def slot_tables(expert_ids, groups):
@@ -42,7 +47,7 @@
     arrived = lax.all_to_all(send_rows, "expert", split_axis=0, concat_axis=0, tiled=True)
     rows_in = arrived.reshape(groups, WAVE, MOST, model_width)
     full_gate, full_up, full_down = (
-        lax.all_gather(w_gate, "fsdp", axis=1, tiled=True),
+        _number_series_all(w_gate, "fsdp"),
         lax.all_gather(w_up, "fsdp", axis=1, tiled=True),
         lax.all_gather(w_down, "fsdp", axis=1, tiled=True),
     )

time: 463 us -> 583 us (1.26); the launches traced: 461 us -> 572 us
  other arithmetic: 33.2 us -> 159 us
  waiting for transfers between devices: 279 us -> 212 us
  local copies, waits for them, and re-layouts: 62.6 us -> 100 us
  matrix products: 53.3 us -> 62.1 us
  starting transfers between devices: 18.3 us -> 25 us
    unnamed x2 -> x3, other arithmetic: 0.09 us -> 124 us
    all_to_all x0 -> x1, waiting for transfers between devices: none -> 72.6 us  [_number_series_all(): lax.all_to_all(kept_arr, axis_name=mesh_dim, split_axis=1, concat_axis=1,...]
    all_gather x1 -> x0, waiting for transfers between devices: 54 us -> none  [on_device(): lax.all_gather(w_gate, 'fsdp', axis=1, tiled=True)]
    all_gather x1, waiting for transfers between devices: 52 us -> 0.01 us  [on_device(): lax.all_gather(w_up, 'fsdp', axis=1, tiled=True)]
    unnamed x25 -> x47, local copies, waits for them, and re-layouts: 6.7 us -> 45 us
    all_gather x1, waiting for transfers between devices: 12.8 us -> 0.01 us  [on_device(): lax.all_gather(w_down, 'fsdp', axis=1, tiled=True)]
    all_to_all x1, waiting for transfers between devices: 12.5 us -> 0.01 us  [on_device(): lax.all_to_all(expert_out.reshape(groups, WAVE * MOST, model_width), 'exp...]
    reduce_scatter x1, waiting for transfers between devices: 26.1 us -> 37.7 us  [on_device(): lax.psum_scatter(term_gate.astype(jnp.bfloat16), 'fsdp', scatter_dimensio...]
  transfers between devices with their start and end apart: 10 -> 10, of which waited for: 9 -> 6; matrix products, arithmetic and copies ran while one was open for 28% -> 52% of each run, Pallas kernels for 0% -> 0%
where the time goes in v1:
time: 583 us; the launch traced here: 572 us
  waiting for transfers between devices  212 us (36%)
  other arithmetic  159 us (27%)
  local copies, waits for them, and re-layouts  100 us (17%)
  matrix products  62.1 us (11%)
  starting transfers between devices  25 us (4%)
  between operations  14.4 us (2%)
    unnamed x3, other arithmetic  124 us
    reduce_scatter x1, waiting for transfers between devices, on_device(): lax.psum_scatter(term_up.astype(jnp.bfloat16), 'fsdp', scatter_dimension=...  80.6 us
    all_to_all x1, waiting for transfers between devices, _number_series_all(): lax.all_to_all(kept_arr, axis_name=mesh_dim, split_axis=1, concat_axis=1,...  72.6 us
    unnamed x47, local copies, waits for them, and re-layouts  45 us
    reduce_scatter x1, waiting for transfers between devices, on_device(): lax.psum_scatter(term_gate.astype(jnp.bfloat16), 'fsdp', scatter_dimensio...  37.7 us
    all_to_all x1, waiting for transfers between devices, on_device(): lax.all_to_all(row_grad.reshape(groups, WAVE * MOST, model_width), 'exper...  13.5 us
    reduce_sum x1, other arithmetic, on_device(): jnp.sum(cotangent.astype(jnp.float32)[:, None, :] * slot_out, axis=2)  12 us
    convert_element_type x1, local copies, waits for them, and re-layouts, on_device(): back_pad[target].reshape(tok_count, TOP, model_width).astype(jnp.float32)  12 us
  transfers between devices with their start and end apart: 10, of which 6 were waited for; matrix products, arithmetic and copies ran while one was open for 52% of the time, Pallas kernels for 0%

profile of v1, /device:TPU:0, one launch (start us, length us, event | category | flops | bytes accessed | tf_op | source)
XLA Modules:
  0.0 572.4 jit_solution(3572169499040377126)
XLA Ops:
  26.3 124.2 %reduce.11 = bf16[2048,1408]{1,0:T(8,128)(2,1)} reduce(bf16[2048,1,1408]{2,1,0:T(2,128)(2,1)} %bitcast.120, bf16[]{:T(256)} %broadcast.343), dimensions={1}, to_apply=%bitcast.109.reduce_sub_computation | reduce | bytes 11534338
  150.5 11.3 %reshape.397 = bf16[16,2,90112]{2,1,0:T(2,128)(2,1)} reshape(bf16[2048,1408]{1,0:T(8,128)(2,1)} %reduce.11) | data formatting | bytes 11534336
  161.8 7.3 %all-to-all-start = ((bf16[16,2,90112]{2,1,0:T(2,128)(2,1)}), bf16[16,2,90112]{2,1,0:T(2,128)(2,1)}, u32[]{:S(2)}, u32[]{:S(2)}) async-start(bf16[16,2,90112]{2,1,0:T(2,128)(2,1)} %reshape.397), calls=%async_computation | async-start | bytes 11534336 | tf_op jit(solution)/shard_map/all_to_all | solution.py:14
  172.9 6.2 %scatter_custom_fusion = s32[384]{0:T(512)S(1)} fusion(s32[1536]{0:T(1024)S(1)} %get-tuple-element.21, s32[1536]{0:T(1024)S(1)} %iota.11, s32[]{:T(128)} %constant.52.clone.1), kind=kCustom, calls=%fused_computation.114 | custom fusion | bytes 1540 | tf_op jit(solution)/shard_map/scatter | solution.py:32
  182.2 72.6 %all-to-all-done = bf16[16,2,90112]{2,1,0:T(2,128)(2,1)} async-done(((bf16[16,2,90112]{2,1,0:T(2,128)(2,1)}), bf16[16,2,90112]{2,1,0:T(2,128)(2,1)}, u32[]{:S(2)}, u32[]{:S(2)}) %all-to-all-start) | async-done | bytes 5767200 | tf_op jit(solution)/shard_map/all_to_all | solution.py:14
  254.8 5.3 all-to-all-start.1
  267.5 13.8 %reshape.398 = bf16[2048,1,1408]{2,1,0:T(2,128)(2,1)} reshape(bf16[16,2,90112]{2,1,0:T(2,128)(2,1)} %all-to-all-done) | data formatting | bytes 11534336
  286.4 8.7 %fusion.17 = f32[8,1,48,1408]{3,2,0,1:T(8,128)} fusion(bf16[8,48,2048]{2,1,0:T(8,128)(2,1)} %all-to-all-done.1, bf16[1,2048,1408]{2,0,1:T(2,128)(2,1)} %bitcast.121), kind=kOutput, calls=%fused_computation.30 | convolution fusion | flops 2214592512 | bytes 9502720 | tf_op jit(solution)/shard_map/skmd,kdf->skmf/dot_general | solution.py:54
  295.0 7.1 %fusion.20 = f32[8,1,48,1408]{3,2,0,1:T(8,128)} fusion(bf16[8,48,2048]{2,1,0:T(8,128)(2,1)} %all-to-all-done.1, bf16[1,2048,1408]{2,1,0:T(8,128)(2,1)} %all-gather.3.cloned.1.call-done), kind=kOutput, calls=%fused_computation.31 | convolution fusion | flops 2214592512 | bytes 9502720 | tf_op jit(solution)/shard_map/skmd,kdf->skmf/dot_general | solution.py:55
  302.1 5.5 all-to-all-done.3
  307.7 7.5 %multiply_convert_fusion = (bf16[8,1,48,1408]{3,2,0,1:T(8,128)(2,1)}, bf16[8,1,48,1408]{3,2,0,1:T(8,128)(2,1)}, bf16[8,1,48,1408]{3,2,0,1:T(8,128)(2,1)S(1)}) fusion(f32[8,1,48,1408]{3,2,0,1:T(8,128)} %fusion.17, f32[8,1,48,1408]{3,2,0,1:T(8,128)} %fusion.20, bf16[8,48,2048]{2,1,0:T(8,128)(2,1)S(1)} %all-to-all-done.3, ...), kind=kOutput, calls=%fused_computation.37 | convolution fusion | flops 2223243264 | bytes 14909440 | tf_op jit(solution)/shard_map/skmd,kdf->skmf/dot_general | solution.py:84
  321.6 7.3 %fusion = bf16[1,2048,1408]{2,1,0:T(8,128)(2,1)} fusion(bf16[8,48,2048]{2,1,0:T(8,128)(2,1)} %all-to-all-done.1, bf16[8,1,48,1408]{3,2,0,1:T(8,128)(2,1)S(1)} %copy-done.10), kind=kOutput, calls=%fused_computation.11 | convolution fusion | flops 2217476096 | bytes 8421376 | tf_op jit(solution)/shard_map/skmd,skmf->kdf/dot_general | solution.py:106
  330.1 7.2 %fusion.1 = bf16[1,2048,1408]{2,1,0:T(8,128)(2,1)} fusion(bf16[8,48,2048]{2,1,0:T(8,128)(2,1)} %all-to-all-done.1, bf16[8,1,48,1408]{3,2,0,1:T(8,128)(2,1)S(1)} %copy-done.8), kind=kOutput, calls=%fused_computation.12 | convolution fusion | flops 2217476096 | bytes 8421376 | tf_op jit(solution)/shard_map/skmd,skmf->kdf/dot_general | solution.py:107
  337.4 7.3 %fusion.3 = f32[2048,8,48]{0,2,1:T(8,128)S(1)} fusion(bf16[1,2048,1408]{2,0,1:T(2,128)(2,1)} %bitcast.122, bf16[8,1,48,1408]{3,2,0,1:T(8,128)(2,1)} %get-tuple-element.23), kind=kOutput, calls=%fused_computation.14 | convolution fusion | flops 2214592512 | bytes 9994240 | tf_op jit(solution)/shard_map/skmf,kdf->skmd/dot_general | solution.py:92
  352.2 8.0 %fusion.28 = bf16[8,48,2048]{2,1,0:T(8,128)(2,1)} fusion(bf16[1,2048,1408]{2,1,0:T(8,128)(2,1)} %all-gather.5.cloned.1.call-done, bf16[8,1,48,1408]{3,2,0,1:T(8,128)(2,1)S(1)} %get-tuple-element.24), kind=kOutput, calls=%fused_computation.33 | convolution fusion | flops 2215378944 | bytes 8421376 | tf_op jit(solution)/shard_map/skmf,kdf->skmd/dot_general | solution.py:58
  360.1 13.5 %all-to-all-done.4 = bf16[8,48,2048]{2,1,0:T(8,128)(2,1)S(1)} async-done(((bf16[8,48,2048]{2,1,0:T(8,128)(2,1)}), bf16[8,48,2048]{2,1,0:T(8,128)(2,1)S(1)}, u32[]{:S(2)}, u32[]{:S(2)}) %all-to-all-start.4) | async-done | bytes 1572896 | tf_op jit(solution)/shard_map/all_to_all | solution.py:95
  382.0 7.0 %gather_fusion.4 = bf16[1536,2048]{1,0:T(8,128)(2,1)} fusion(bf16[385,2048]{1,0:T(8,128)(2,1)S(1)} %concatenate.23, s32[2048]{0:T(1024)S(1)} %pad_clamp_fusion), kind=kCustom, calls=%fused_computation.4 | custom fusion | bytes 12589056 | tf_op jit(solution)/shard_map/gather | solution.py:104
  389.0 11.0 %reshape.330 = bf16[256,6,2048]{2,1,0:T(8,128)(2,1)} reshape(bf16[1536,2048]{1,0:T(8,128)(2,1)} %gather_fusion.4) | data formatting | bytes 12582912 | tf_op jit(solution)/shard_map/reshape | solution.py:104
  400.0 9.7 %reduce_sum.44 = bf16[256,2048]{1,0:T(8,128)(2,1)} reduce(bf16[256,6,2048]{2,1,0:T(8,128)(2,1)} %reshape.330, bf16[]{:T(256)} %constant.31.clone.1), dimensions={1}, to_apply=%region_5.6 | reduce | flops 2621440 | bytes 7340034 | tf_op jit(solution)/shard_map/reduce_sum | solution.py:103
  410.0 7.1 %gather_fusion.1 = bf16[1536,2048]{1,0:T(8,128)(2,1)} fusion(bf16[385,2048]{1,0:T(8,128)(2,1)S(1)} %concatenate.20, s32[2048]{0:T(1024)S(1)} %pad_clamp_fusion), kind=kCustom, calls=%fused_computation.1 | custom fusion | bytes 12589056 | tf_op jit(solution)/shard_map/gather | solution.py:69
  417.0 12.0 %reshape.331 = f32[256,6,2048]{2,1,0:T(8,128)} reshape(bf16[1536,2048]{1,0:T(8,128)(2,1)} %gather_fusion.1) | data formatting | bytes 18874368 | tf_op jit(solution)/shard_map/convert_element_type | solution.py:69
  429.0 12.0 %multiply_reduce_fusion = (f32[256,6]{1,0:T(8,128)S(1)}, bf16[256,2048]{1,0:T(8,128)(2,1)}) fusion(f32[256,6,2048]{2,1,0:T(8,128)} %reshape.331, f32[256,2048]{1,0:T(8,128)S(1)} %copy-done.2, f32[256,6]{1,0:T(8,128)S(1)} %copy.41), kind=kLoop, calls=%fused_computation.6 | loop fusion | flops 12057088 | bytes 15740928 | tf_op jit(solution)/shard_map/reduce_sum | solution.py:73
  443.6 37.7 %reduce-scatter.4.cloned.1.call-done = bf16[1,128,1408]{2,1,0:T(8,128)(2,1)} async-done(((bf16[1,2048,1408]{2,1,0:T(8,128)(2,1)}), bf16[1,128,1408]{2,1,0:T(8,128)(2,1)}) %reduce-scatter.4.cloned.1.call-update) | async-done | bytes 360464 | tf_op jit(solution)/shard_map/reduce_scatter | solution.py:110
  483.2 80.6 %reduce-scatter.6.cloned.1.call-done = bf16[1,128,1408]{2,1,0:T(8,128)(2,1)} async-done(((bf16[1,2048,1408]{2,1,0:T(8,128)(2,1)}), bf16[1,128,1408]{2,1,0:T(8,128)(2,1)}) %reduce-scatter.6.cloned.1.call-update) | async-done | bytes 360464 | tf_op jit(solution)/shard_map/reduce_scatter | solution.py:113
  (99 shorter events, 67.9 us)
Async XLA Ops:
  7.2 6.2 %copy-start = (bf16[1,128,1408]{2,1,0:T(8,128)(2,1)S(1)}, bf16[1,128,1408]{2,1,0:T(8,128)(2,1)}, u32[]{:S(2)}) copy-start(bf16[1,128,1408]{2,1,0:T(8,128)(2,1)} %param.10) | copy-start | bytes 1081348
  7.2 287.9 %all-gather.3.cloned.1.call-start = ((), (), s32[]{:S(2)}) async-start(), calls=%async_computation.8 | async-start | bytes 6127616 | tf_op jit(solution)/shard_map/all_gather | solution.py:51
  7.9 299.8 %all-gather.5.cloned.1.call-start = ((), (), s32[]{:S(2)}) async-start(), calls=%async_computation.9 | async-start | bytes 6127616 | tf_op jit(solution)/shard_map/all_gather | solution.py:52
  21.4 4.3 copy-start.1
  161.8 7.3 %copy-start.7 = (s32[256,6]{0,1:T(8,128)S(1)}, s32[256,6]{0,1:T(8,128)}, u32[]{:S(2)}) copy-start(s32[256,6]{0,1:T(8,128)} %param.8) | copy-start | bytes 18436
  161.8 10.7 %copy-start.5 = (bf16[256,2048]{1,0:T(8,128)(2,1)S(1)}, bf16[256,2048]{1,0:T(8,128)(2,1)}, u32[]{:S(2)}) copy-start(bf16[256,2048]{1,0:T(8,128)(2,1)} %param.7) | copy-start | bytes 3145732
  161.8 93.0 %all-to-all-start = ((bf16[16,2,90112]{2,1,0:T(2,128)(2,1)}), bf16[16,2,90112]{2,1,0:T(2,128)(2,1)}, u32[]{:S(2)}, u32[]{:S(2)}) async-start(bf16[16,2,90112]{2,1,0:T(2,128)(2,1)} %reshape.397), calls=%async_computation | async-start | bytes 11534336 | tf_op jit(solution)/shard_map/all_to_all | solution.py:14
  182.2 77.9 %copy-start.4 = (bf16[256,2048]{1,0:T(8,128)(2,1)S(1)}, bf16[256,2048]{1,0:T(8,128)(2,1)}, u32[]{:S(2)}) copy-start(bf16[256,2048]{1,0:T(8,128)(2,1)} %param.13) | copy-start | bytes 3145732
  254.8 27.0 %all-to-all-start.1 = ((bf16[8,48,2048]{2,1,0:T(8,128)(2,1)}), bf16[8,48,2048]{2,1,0:T(8,128)(2,1)}, u32[]{:S(2)}, u32[]{:S(2)}) async-start(bf16[8,48,2048]{2,1,0:T(8,128)(2,1)} %bitcast.1), calls=%async_computation.1 | async-start | bytes 3145728 | tf_op jit(solution)/shard_map/all_to_all | solution.py:47
  260.3 2.5 copy-start.6
  281.8 25.8 %all-to-all-start.3 = ((bf16[8,48,2048]{2,1,0:T(8,128)(2,1)}), bf16[8,48,2048]{2,1,0:T(8,128)(2,1)S(1)}, u32[]{:S(2)}, u32[]{:S(2)}) async-start(bf16[8,48,2048]{2,1,0:T(8,128)(2,1)} %fusion.15), calls=%async_computation.3 | async-start | bytes 3145728 | tf_op jit(solution)/shard_map/all_to_all | solution.py:76
  286.1 155.6 %reduce-scatter.8.cloned.1.call-start = ((), (), s32[]{:S(2)}) async-start(), calls=%async_computation.12 | async-start | bytes 6127616 | tf_op jit(solution)/shard_map/reduce_scatter | solution.py:116
  320.4 1.2 copy-start.10
  320.4 160.9 %reduce-scatter.4.cloned.1.call-start = ((), (), s32[]{:S(2)}) async-start(), calls=%async_computation.10 | async-start | bytes 6127616 | tf_op jit(solution)/shard_map/reduce_scatter | solution.py:110
  328.9 1.2 copy-start.8
  328.9 234.9 %reduce-scatter.6.cloned.1.call-start = ((), (), s32[]{:S(2)}) async-start(), calls=%async_computation.11 | async-start | bytes 6127616 | tf_op jit(solution)/shard_map/reduce_scatter | solution.py:113
  337.3 7.4 %slice-start = ((s8[5767168]{0:T(1024)(128)(4,1)}), s8[1572864]{0:T(1024)(128)(4,1)S(1)}, s32[]{:S(2)}) async-start(s8[5767168]{0:T(1024)(128)(4,1)} %bitcast.127), calls=%async_computation.13 | async-start | bytes 3145728
  337.4 7.4 %slice-start.1 = ((s8[5767168]{0:T(1024)(128)(4,1)}), s8[4194304]{0:T(1024)(128)(4,1)S(1)}, s32[]{:S(2)}) async-start(s8[5767168]{0:T(1024)(128)(4,1)} %bitcast.127), calls=%async_computation.14 | async-start | bytes 8388608
  337.4 7.4 %copy-start.9 = (bf16[8,1,48,1408]{3,2,0,1:T(8,128)(2,1)S(1)}, bf16[8,1,48,1408]{3,2,0,1:T(8,128)(2,1)}, u32[]{:S(2)}) copy-start(bf16[8,1,48,1408]{3,2,0,1:T(8,128)(2,1)} %get-tuple-element.22) | copy-start | bytes 3244036
  348.6 25.1 %all-to-all-start.4 = ((bf16[8,48,2048]{2,1,0:T(8,128)(2,1)}), bf16[8,48,2048]{2,1,0:T(8,128)(2,1)S(1)}, u32[]{:S(2)}, u32[]{:S(2)}) async-start(bf16[8,48,2048]{2,1,0:T(8,128)(2,1)} %fusion.31), calls=%async_computation.4 | async-start | bytes 3145728 | tf_op jit(solution)/shard_map/all_to_all | solution.py:95
  373.7 6.6 %copy-start.3 = (bf16[8,48,2048]{2,1,0:T(8,128)(2,1)}, bf16[8,48,2048]{2,1,0:T(8,128)(2,1)S(1)}, u32[]{:S(2)}) copy-start(bf16[8,48,2048]{2,1,0:T(8,128)(2,1)S(1)} %all-to-all-done.4) | copy-start | bytes 4718596
  373.7 36.1 %all-to-all-start.2 = ((bf16[8,48,2048]{2,1,0:T(8,128)(2,1)}), bf16[8,48,2048]{2,1,0:T(8,128)(2,1)S(1)}, u32[]{:S(2)}, u32[]{:S(2)}) async-start(bf16[8,48,2048]{2,1,0:T(8,128)(2,1)} %fusion.28), calls=%async_computation.2 | async-start | bytes 3145728 | tf_op jit(solution)/shard_map/all_to_all | solution.py:61
  417.0 12.0 %copy-start.2 = (f32[256,2048]{1,0:T(8,128)S(1)}, f32[256,2048]{1,0:T(8,128)}, u32[]{:S(2)}) copy-start(f32[256,2048]{1,0:T(8,128)} %convert_element_type.115) | copy-start | bytes 6291460
Sparse Core Ops, SparseCore 0:
  10.1 61.1 all-gather.2
  73.5 58.4 all-gather.4
  320.5 78.1 reduce-scatter.7
  402.0 79.2 reduce-scatter.3
  484.5 79.2 reduce-scatter.5
